TPU v7x, 256 devices: a whole 4x4x8 slice. The times are simulated.
256 devices in a mesh: section: 4 (over z_hi), seq: 64 (over x, y, z_lo, core).
Axes of the slice: x: 4, y: 4, z: 8 (z_hi: 4, z_lo: 2; z = z_hi * 2 + z_lo), core: 2. Of those that a mesh axis runs over, the one named last changes fastest.
Arguments:
- memory: bfloat16 [8, 4096, 4096], P(None, 'seq', 'section'), may hold values from -6 to 6
- kv_weight: bfloat16 [4096, 4096], P('seq', 'section'), may hold values from -0.09375 to 0.09375
- mem_lengths: int32 [8], replicated, may hold values from 1024 to 4096, as said below
- queries: bfloat16 [16384, 2048], P('seq', 'section'), may hold values from -128 to 128
- out_weight: bfloat16 [2048, 4096], P('section'), may hold values from -0.125 to 0.125
- residual: bfloat16 [16384, 4096], P(('seq', 'section')), may hold values from -1.5 to 1.5
- norm_gain: float32 [4096], replicated, may hold values from 0.5 to 1.5
Outputs:
- hidden_out: bfloat16 [16384, 4096], P(('seq', 'section'))
- normed_out: bfloat16 [16384, 4096], P(('seq', 'section'))
Inputs may be any that keep to these rules, and one draw needn't show every extreme that they name: `mem_lengths`: valid memory positions of each proof state; positions at or beyond it are padding; at least one proof state has none.
All inputs are finite; a program needn't handle non-finite values.
Results may differ from a plain program's by a relative error of at most 0.012.
Values may be sent and summed in bfloat16 or wider, within the bound.
No kernel may reach another device: no remote copies, remote signals or barrier semaphores. Data moves between devices by JAX's collectives and lax.ppermute only.
A program may use at most 128 MiB of HBM per device.

v0:
```python
import math
import jax
import jax.numpy as jnp
from jax import lax
from jax.sharding import PartitionSpec as P

DH = 256


def project_rows(mem_rows, kv_weight):
    summed = jnp.dot(
        mem_rows,
        lax.all_gather(kv_weight, "seq", axis=0, tiled=True),
        preferred_element_type=jnp.float32,
    )
    return summed.astype(jnp.bfloat16)


def shards(memory, kv_weight, mem_lengths, queries, out_weight, residual, norm_gain):
    seq_count = lax.axis_size("seq")
    states = memory.shape[0]
    group = seq_count // states
    local_heads = queries.shape[1] // DH
    widened = lax.all_gather(memory, "section", axis=2, tiled=True)
    block_len = widened.shape[1]
    feature_count = widened.shape[2]
    projected = project_rows(widened.reshape(states * block_len, feature_count), kv_weight)
    projected = projected.reshape(states, block_len, projected.shape[1])
    spread = jnp.repeat(projected, group, axis=0)
    key_value = lax.all_to_all(spread, "seq", split_axis=0, concat_axis=1, tiled=True)[0]
    state_index = lax.axis_index("seq") // group
    length = lax.dynamic_index_in_dim(mem_lengths, state_index, 0, keepdims=False)
    memory_len = key_value.shape[0]
    split_heads = key_value.reshape(memory_len, local_heads, 2, DH)
    shard_key_rows = split_heads[:, :, 0, :]
    shard_value_rows = split_heads[:, :, 1, :]
    query_per_head = queries.reshape(queries.shape[0], local_heads, DH)
    logit_scores = jnp.einsum(
        "wac,oac->awo", query_per_head, shard_key_rows, preferred_element_type=jnp.float32
    )
    logit_scores = logit_scores * (1.0 / math.sqrt(DH))
    visible = jnp.arange(memory_len, dtype=jnp.int32) < length
    logit_scores = jnp.where(visible[None, None, :], logit_scores, -1e30)
    highest = jnp.max(logit_scores, axis=-1, keepdims=True)
    expo = jnp.exp(logit_scores - highest)
    softmax_weight = (expo / jnp.sum(expo, axis=-1, keepdims=True)).astype(jnp.bfloat16)
    attended_context = jnp.einsum(
        "fsw,wfy->sfy", softmax_weight, shard_value_rows, preferred_element_type=jnp.float32
    )
    attended_context = attended_context.astype(jnp.bfloat16).reshape(
        query_per_head.shape[0], local_heads * DH
    )
    attended = lax.psum_scatter(
        jnp.dot(attended_context, out_weight, preferred_element_type=jnp.float32),
        "section",
        scatter_dimension=0,
        tiled=True,
    )
    combined = residual.astype(jnp.float32) + attended
    mean_square = jnp.mean(combined * combined, axis=-1, keepdims=True)
    normed = combined * lax.rsqrt(mean_square + 1e-06) * norm_gain
    return (combined.astype(jnp.bfloat16), normed.astype(jnp.bfloat16))


def solution(mesh):
    in_specs = (
        P(None, "seq", "section"),
        P("seq", "section"),
        P(),
        P("seq", "section"),
        P("section", None),
        P(("seq", "section"), None),
        P(),
    )
    out_specs = (P(("seq", "section"), None), P(("seq", "section"), None))
    return jax.shard_map(shards, mesh=mesh, in_specs=in_specs, out_specs=out_specs, check_vma=False)
```

profile of v0, /device:TPU:1, one launch (start us, length us, event | category | flops | bytes accessed | tf_op | source)
XLA Modules:
  0.0 516.3 jit_solution(13996166611527082985)
XLA Ops:
  7.2 0.0 all-gather.3.cloned.1.call-start
  7.2 0.7 all-gather.3.cloned.1.call-update
  7.9 0.0 all-gather.5.cloned.1.call-start
  7.9 0.7 all-gather.5.cloned.1.call-update
  8.6 80.3 %all-gather.3.cloned.1.call-done = bf16[8,64,4096]{2,1,0:T(8,128)(2,1)} async-done(((bf16[8,64,1024]{2,1,0:T(8,128)(2,1)}), bf16[8,64,4096]{2,1,0:T(8,128)(2,1)}) %all-gather.3.cloned.1.call-update) | async-done | bytes 4194320 | tf_op jit(solution)/shard_map/all_gather | solution.py:24
  89.0 124.5 %all-gather.5.cloned.1.call-done = bf16[4096,1024]{1,0:T(8,128)(2,1)} async-done(((bf16[64,1024]{1,0:T(8,128)(2,1)}), bf16[4096,1024]{1,0:T(8,128)(2,1)}) %all-gather.5.cloned.1.call-update) | async-done | bytes 8388624 | tf_op jit(solution)/shard_map/all_gather | solution.py:13
  213.5 9.1 %convolution_convert_fusion = bf16[512,1024]{1,0:T(8,128)(2,1)S(1)} fusion(bf16[512,4096]{1,0:T(8,128)(2,1)} %bitcast.38, bf16[4096,1024]{1,0:T(8,128)(2,1)} %all-gather.5.cloned.1.call-done), kind=kOutput, calls=%fused_computation.14 | convolution fusion | flops 4295491584 | bytes 13631488 | tf_op jit(solution)/shard_map/dot_general | solution.py:11
  222.6 4.3 broadcast_in_dim.20
  226.9 6.5 %all-to-all-start = ((bf16[64,64,1024]{2,1,0:T(8,128)(2,1)}), bf16[64,64,1024]{2,1,0:T(8,128)(2,1)}, u32[]{:S(2)}, u32[]{:S(2)}) async-start(bf16[64,64,1024]{2,1,0:T(8,128)(2,1)} %bitcast.34), calls=%async_computation | async-start | bytes 16777216 | tf_op jit(solution)/shard_map/all_to_all | solution.py:30
  233.5 0.2 reduce-scatter.2.cloned.1.call-start
  233.7 0.6 dynamic_slice.4
  234.3 0.7 iota_compare_fusion
  235.0 102.5 %all-to-all-done = bf16[64,64,1024]{2,1,0:T(8,128)(2,1)} async-done(((bf16[64,64,1024]{2,1,0:T(8,128)(2,1)}), bf16[64,64,1024]{2,1,0:T(8,128)(2,1)}, u32[]{:S(2)}, u32[]{:S(2)}) %all-to-all-start) | async-done | bytes 8388640 | tf_op jit(solution)/shard_map/all_to_all | solution.py:30
  337.5 14.5 %reshape_squeeze.3 = bf16[4096,2,2,256]{3,2,1,0:T(2,128)(2,1)} reshape(bf16[64,64,1024]{2,1,0:T(8,128)(2,1)} %all-to-all-done) | data formatting | bytes 16777216 | tf_op jit(solution)/shard_map/reshape;squeeze | solution.py:34
  351.9 17.3 %fusion.19 = (bf16[4096,2,1,256]{3,2,1,0:T(2,128)(2,1)}, bf16[4096,2,1,256]{3,2,1,0:T(2,128)(2,1)}) fusion(bf16[4096,2,2,256]{3,2,1,0:T(2,128)(2,1)} %reshape_squeeze.3), kind=kLoop, calls=%fused_computation.26 | loop fusion | bytes 16777216 | tf_op jit(solution)/shard_map/slice | solution.py:36
  369.3 18.5 %copy.17 = bf16[4096,2,1,256]{0,3,1,2:T(8,128)(2,1)} copy(bf16[4096,2,1,256]{3,2,1,0:T(2,128)(2,1)} %get-tuple-element.2) | data formatting | bytes 8388608
  387.8 4.7 fusion.5
  392.5 6.0 %fusion.20 = (f32[2,256]{1,0:T(2,128)S(1)}, f32[2,256,4096]{1,2,0:T(8,128)}) fusion(f32[2,4096,256]{2,1,0:T(8,128)S(1)} %fusion.5, pred[4096]{0:T(1024)(128)(4,1)S(1)} %iota_compare_fusion), kind=kOutput, calls=%fused_computation.27 | output fusion | flops 12587007 | bytes 16783360 | tf_op jit(solution)/shard_map/sub | solution.py:45
  398.5 4.9 fusion.11
  403.4 3.2 fusion.21
  406.6 0.0 reduce-scatter.2.cloned.1.call-update
  406.7 99.2 %reduce-scatter.2.cloned.1.call-done = f32[64,4096]{1,0:T(8,128)} async-done(((f32[256,4096]{1,0:T(8,128)}), f32[64,4096]{1,0:T(8,128)}) %reduce-scatter.2.cloned.1.call-update) | async-done | bytes 1048592 | tf_op jit(solution)/shard_map/reduce_scatter | solution.py:53
  505.8 1.5 multiply_reduce_fusion
  507.3 2.4 multiply_convert_fusion
  (13 shorter events, 0.0 us)
Async XLA Ops:
  7.2 81.8 %all-gather.3.cloned.1.call-start = ((), (), s32[]{:S(2)}) async-start(), calls=%async_computation.2 | async-start | bytes 5242880 | tf_op jit(solution)/shard_map/all_gather | solution.py:24
  7.9 205.6 %all-gather.5.cloned.1.call-start = ((), (), s32[]{:S(2)}) async-start(), calls=%async_computation.3 | async-start | bytes 8519680 | tf_op jit(solution)/shard_map/all_gather | solution.py:13
  226.9 6.8 %copy-start.5 = (s32[8]{0:T(128)S(1)}, s32[8]{0:T(128)}, u32[]{:S(2)}) copy-start(s32[8]{0:T(128)} %param.9) | copy-start | bytes 100
  226.9 110.5 %all-to-all-start = ((bf16[64,64,1024]{2,1,0:T(8,128)(2,1)}), bf16[64,64,1024]{2,1,0:T(8,128)(2,1)}, u32[]{:S(2)}, u32[]{:S(2)}) async-start(bf16[64,64,1024]{2,1,0:T(8,128)(2,1)} %bitcast.34), calls=%async_computation | async-start | bytes 16777216 | tf_op jit(solution)/shard_map/all_to_all | solution.py:30
  233.5 272.4 %reduce-scatter.2.cloned.1.call-start = ((), (), s32[]{:S(2)}) async-start(), calls=%async_computation.4 | async-start | bytes 5242880 | tf_op jit(solution)/shard_map/reduce_scatter | solution.py:53
  369.3 18.5 %copy-start.3 = (bf16[256,512]{1,0:T(8,128)(2,1)S(1)}, bf16[256,512]{1,0:T(8,128)(2,1)}, u32[]{:S(2)}) copy-start(bf16[256,512]{1,0:T(8,128)(2,1)} %param.10) | copy-start | bytes 786436
  392.4 6.0 %copy-start.1 = (bf16[4096,2,1,256]{0,3,1,2:T(8,128)(2,1)S(1)}, bf16[4096,2,1,256]{0,3,1,2:T(8,128)(2,1)}, u32[]{:S(2)}) copy-start(bf16[4096,2,1,256]{0,3,1,2:T(8,128)(2,1)} %copy.17) | copy-start | bytes 12582916
  398.5 4.9 copy-start
  403.4 102.5 %copy-start.2 = (bf16[64,4096]{1,0:T(8,128)(2,1)S(1)}, bf16[64,4096]{1,0:T(8,128)(2,1)}, u32[]{:S(2)}) copy-start(bf16[64,4096]{1,0:T(8,128)(2,1)} %param.12) | copy-start | bytes 1572868
  403.4 104.0 %copy-start.4 = (f32[4096]{0:T(1024)S(1)}, f32[4096]{0:T(1024)}, u32[]{:S(2)}) copy-start(f32[4096]{0:T(1024)} %param.13) | copy-start | bytes 49156
Sparse Core Ops, SparseCore 0:
  9.8 79.1 all-gather.2
  90.8 122.6 all-gather.4
  406.8 99.0 reduce-scatter.1
where the time goes:
time: 517 us; the launch traced here: 516 us
  waiting for transfers between devices  408 us (79%)
  local copies, waits for them, and re-layouts  55.2 us (11%)
  matrix products  21.9 us (4%)
  between operations  13.9 us (3%)
  other arithmetic  10.5 us (2%)
  starting transfers between devices  6.81 us (1%)
    all_gather x1, waiting for transfers between devices, project_rows(): lax.all_gather(kv_weight, 'seq', axis=0, tiled=True)  125 us
    all_to_all x1, waiting for transfers between devices, shards(): lax.all_to_all(spread, 'seq', split_axis=0, concat_axis=1, tiled=True)[0]  102 us
    reduce_scatter x1, waiting for transfers between devices, shards(): lax.psum_scatter(jnp.dot(attended_context, out_weight, preferred_element_...  99.2 us
    all_gather x1, waiting for transfers between devices, shards(): widened = lax.all_gather(memory, 'section', axis=2, tiled=True)  80.3 us
    unnamed x13, local copies, waits for them, and re-layouts  18.5 us
    slice x1, local copies, waits for them, and re-layouts, shards(): shard_value_rows = split_heads[:, :, 1, :]  17.3 us
    another operation x1, local copies, waits for them, and re-layouts, shards(): split_heads = key_value.reshape(memory_len, local_heads, 2, DH)  14.5 us
  transfers between devices with their start and end apart: 4, of which 4 were waited for; matrix products, arithmetic and copies ran while one was open for 0% of the time, Pallas kernels for 0%

commit v1 on v0

--- a/solution.py
+++ b/solution.py
@@ -21,7 +21,10 @@
     states = memory.shape[0]
     group = seq_count // states
     local_heads = queries.shape[1] // DH
-    widened = lax.all_gather(memory, "section", axis=2, tiled=True)
+    widened = jnp.concatenate(
+        lax.all_to_all(jnp.stack([memory] * lax.axis_size("section"), axis=0), "section", 0, 0),
+        axis=2,
+    )
     block_len = widened.shape[1]
     feature_count = widened.shape[2]
     projected = project_rows(widened.reshape(states * block_len, feature_count), kv_weight)

time: 517 us -> 462 us (0.89)
  waiting for transfers between devices: 408 us -> 198 us
  blocking collectives: 0 us -> 144 us
  local copies, waits for them, and re-layouts: 55.2 us -> 64.3 us
    all_to_all x0 -> x1, blocking collectives: none -> 144 us  [shards(): lax.all_to_all(jnp.stack([memory] * lax.axis_size('section'), axis=0), 's...]
    all_gather x1, waiting for transfers between devices: 125 us -> 0.01 us  [project_rows(): lax.all_gather(kv_weight, 'seq', axis=0, tiled=True)]
    all_gather x1 -> x0, waiting for transfers between devices: 80.3 us -> none  [shards(): widened = lax.all_gather(memory, 'section', axis=2, tiled=True)]
    reduce_scatter x1, waiting for transfers between devices: 99.2 us -> 94 us  [shards(): lax.psum_scatter(jnp.dot(attended_context, out_weight, preferred_element_...]
    unnamed x13 -> x14, local copies, waits for them, and re-layouts: 18.5 us -> 22.8 us
  transfers between devices with their start and end apart: 4 -> 3, of which waited for: 4 -> 2; matrix products, arithmetic and copies ran while one was open for 0% -> 2% of each run, Pallas kernels for 0% -> 0%
where the time goes in v1:
time: 462 us; the launch traced here: 461 us
  waiting for transfers between devices  198 us (43%)
  blocking collectives  144 us (31%)
  local copies, waits for them, and re-layouts  64.3 us (14%)
  matrix products  21.9 us (5%)
  between operations  14.2 us (3%)
  other arithmetic  10.5 us (2%)
  starting transfers between devices  8.85 us (2%)
    all_to_all x1, blocking collectives, shards(): lax.all_to_all(jnp.stack([memory] * lax.axis_size('section'), axis=0), 's...  144 us
    all_to_all x1, waiting for transfers between devices, shards(): lax.all_to_all(spread, 'seq', split_axis=0, concat_axis=1, tiled=True)[0]  103 us
    reduce_scatter x1, waiting for transfers between devices, shards(): lax.psum_scatter(jnp.dot(attended_context, out_weight, preferred_element_...  94 us
    unnamed x14, local copies, waits for them, and re-layouts  22.8 us
    slice x1, local copies, waits for them, and re-layouts, shards(): shard_value_rows = split_heads[:, :, 1, :]  17.2 us
    another operation x1, local copies, waits for them, and re-layouts, shards(): split_heads = key_value.reshape(memory_len, local_heads, 2, DH)  14.4 us
  transfers between devices with their start and end apart: 3, of which 2 were waited for; matrix products, arithmetic and copies ran while one was open for 2% of the time, Pallas kernels for 0%

profile of v1, /device:TPU:1, one launch (start us, length us, event | category | flops | bytes accessed | tf_op | source)
XLA Modules:
  0.0 461.2 jit_solution(2233285493416272345)
XLA Ops:
  7.2 0.0 all-gather.2.cloned.1.call-start
  7.2 0.7 all-gather.2.cloned.1.call-update
  7.9 1.7 stack.2
  9.6 143.8 %all_to_all.14 = bf16[4,8,64,1024]{3,2,1,0:T(8,128)(2,1)S(1)} all-to-all(bf16[4,8,64,1024]{3,2,1,0:T(8,128)(2,1)S(1)} %stack.2), channel_id=1, replica_groups=mesh['section'=4,'seq'=64] {'section'}, dimensions={0} | all-to-all | bytes 8388608 | tf_op jit(solution)/shard_map/all_to_all | solution.py:25
  153.5 3.3 copy.16
  156.7 4.3 copy.25
  161.0 9.1 %convolution_convert_fusion = bf16[512,1024]{1,0:T(8,128)(2,1)S(1)} fusion(bf16[512,4096]{1,0:T(8,128)(2,1)} %bitcast.40, bf16[4096,1024]{1,0:T(8,128)(2,1)} %all-gather.2.cloned.1.call-done), kind=kOutput, calls=%fused_computation.14 | convolution fusion | flops 4295491584 | bytes 13631488 | tf_op jit(solution)/shard_map/dot_general | solution.py:11
  170.2 4.3 broadcast_in_dim.20
  174.5 8.6 %all-to-all-start.1 = ((bf16[64,64,1024]{2,1,0:T(8,128)(2,1)}), bf16[64,64,1024]{2,1,0:T(8,128)(2,1)}, u32[]{:S(2)}, u32[]{:S(2)}) async-start(bf16[64,64,1024]{2,1,0:T(8,128)(2,1)} %bitcast.37), calls=%async_computation.1 | async-start | bytes 16777216 | tf_op jit(solution)/shard_map/all_to_all | solution.py:33
  183.1 0.2 reduce-scatter.2.cloned.1.call-start
  183.3 0.6 dynamic_slice.4
  183.9 0.7 iota_compare_fusion
  184.6 102.9 %all-to-all-done.1 = bf16[64,64,1024]{2,1,0:T(8,128)(2,1)} async-done(((bf16[64,64,1024]{2,1,0:T(8,128)(2,1)}), bf16[64,64,1024]{2,1,0:T(8,128)(2,1)}, u32[]{:S(2)}, u32[]{:S(2)}) %all-to-all-start.1) | async-done | bytes 8388640 | tf_op jit(solution)/shard_map/all_to_all | solution.py:33
  287.5 14.4 %reshape_squeeze.3 = bf16[4096,2,2,256]{3,2,1,0:T(2,128)(2,1)} reshape(bf16[64,64,1024]{2,1,0:T(8,128)(2,1)} %all-to-all-done.1) | data formatting | bytes 16777216 | tf_op jit(solution)/shard_map/reshape;squeeze | solution.py:37
  301.9 17.2 %fusion.19 = (bf16[4096,2,1,256]{3,2,1,0:T(2,128)(2,1)}, bf16[4096,2,1,256]{3,2,1,0:T(2,128)(2,1)}) fusion(bf16[4096,2,2,256]{3,2,1,0:T(2,128)(2,1)} %reshape_squeeze.3), kind=kLoop, calls=%fused_computation.26 | loop fusion | bytes 16777216 | tf_op jit(solution)/shard_map/slice | solution.py:39
  319.1 18.4 %copy.22 = bf16[4096,2,1,256]{0,3,1,2:T(8,128)(2,1)} copy(bf16[4096,2,1,256]{3,2,1,0:T(2,128)(2,1)} %get-tuple-element.2) | data formatting | bytes 8388608
  337.6 4.7 %fusion.5 = f32[2,4096,256]{2,1,0:T(8,128)S(1)} fusion(bf16[4096,2,1,256]{3,2,1,0:T(2,128)(2,1)} %get-tuple-element.3, bf16[32,2,8,256]{3,2,1,0:T(8,128)(2,1)S(1)} %bitcast.43), kind=kOutput, calls=%fused_computation.8 | convolution fusion | flops 1073741824 | bytes 12845056 | tf_op jit(solution)/shard_map/wac,oac->awo/dot_general | solution.py:41
  342.3 6.0 %fusion.20 = (f32[2,256]{1,0:T(2,128)S(1)}, f32[2,256,4096]{1,2,0:T(8,128)}) fusion(f32[2,4096,256]{2,1,0:T(8,128)S(1)} %fusion.5, pred[4096]{0:T(1024)(128)(4,1)S(1)} %iota_compare_fusion), kind=kOutput, calls=%fused_computation.27 | output fusion | flops 12587007 | bytes 16783360 | tf_op jit(solution)/shard_map/sub | solution.py:48
  348.3 4.9 %fusion.11 = bf16[2,256,256]{2,1,0:T(8,128)(2,1)S(1)} fusion(f32[2,256,4096]{1,2,0:T(8,128)} %get-tuple-element.7, f32[2,256]{1,0:T(2,128)S(1)} %get-tuple-element.6, bf16[4096,2,1,256]{0,3,1,2:T(8,128)(2,1)S(1)} %copy-done.1), kind=kOutput, calls=%fused_computation.15 | convolution fusion | flops 1078067200 | bytes 12847104 | tf_op jit(solution)/shard_map/fsw,wfy->sfy/dot_general | solution.py:50
  353.2 3.2 fusion.21
  356.5 0.0 reduce-scatter.2.cloned.1.call-update
  356.5 94.0 %reduce-scatter.2.cloned.1.call-done = f32[64,4096]{1,0:T(8,128)} async-done(((f32[256,4096]{1,0:T(8,128)}), f32[64,4096]{1,0:T(8,128)}) %reduce-scatter.2.cloned.1.call-update) | async-done | bytes 1048592 | tf_op jit(solution)/shard_map/reduce_scatter | solution.py:56
  450.5 1.5 multiply_reduce_fusion
  452.0 2.4 multiply_convert_fusion
  (14 shorter events, 0.0 us)
Async XLA Ops:
  7.2 153.9 %all-gather.2.cloned.1.call-start = ((), (), s32[]{:S(2)}) async-start(), calls=%async_computation.3 | async-start | bytes 8519680 | tf_op jit(solution)/shard_map/all_gather | solution.py:13
  174.5 8.8 %copy-start.5 = (s32[8]{0:T(128)S(1)}, s32[8]{0:T(128)}, u32[]{:S(2)}) copy-start(s32[8]{0:T(128)} %param.9) | copy-start | bytes 100
  174.5 113.0 %all-to-all-start.1 = ((bf16[64,64,1024]{2,1,0:T(8,128)(2,1)}), bf16[64,64,1024]{2,1,0:T(8,128)(2,1)}, u32[]{:S(2)}, u32[]{:S(2)}) async-start(bf16[64,64,1024]{2,1,0:T(8,128)(2,1)} %bitcast.37), calls=%async_computation.1 | async-start | bytes 16777216 | tf_op jit(solution)/shard_map/all_to_all | solution.py:33
  183.1 267.4 %reduce-scatter.2.cloned.1.call-start = ((), (), s32[]{:S(2)}) async-start(), calls=%async_computation.4 | async-start | bytes 5242880 | tf_op jit(solution)/shard_map/reduce_scatter | solution.py:56
  319.1 18.5 %copy-start.3 = (bf16[256,512]{1,0:T(8,128)(2,1)S(1)}, bf16[256,512]{1,0:T(8,128)(2,1)}, u32[]{:S(2)}) copy-start(bf16[256,512]{1,0:T(8,128)(2,1)} %param.10) | copy-start | bytes 786436
  342.3 6.0 %copy-start.1 = (bf16[4096,2,1,256]{0,3,1,2:T(8,128)(2,1)S(1)}, bf16[4096,2,1,256]{0,3,1,2:T(8,128)(2,1)}, u32[]{:S(2)}) copy-start(bf16[4096,2,1,256]{0,3,1,2:T(8,128)(2,1)} %copy.22) | copy-start | bytes 12582916
  348.3 4.9 %copy-start = (bf16[512,4096]{1,0:T(8,128)(2,1)S(1)}, bf16[512,4096]{1,0:T(8,128)(2,1)}, u32[]{:S(2)}) copy-start(bf16[512,4096]{1,0:T(8,128)(2,1)} %param.11) | copy-start | bytes 12582916
  353.2 97.3 %copy-start.2 = (bf16[64,4096]{1,0:T(8,128)(2,1)S(1)}, bf16[64,4096]{1,0:T(8,128)(2,1)}, u32[]{:S(2)}) copy-start(bf16[64,4096]{1,0:T(8,128)(2,1)} %param.12) | copy-start | bytes 1572868
  353.2 98.8 %copy-start.4 = (f32[4096]{0:T(1024)S(1)}, f32[4096]{0:T(1024)}, u32[]{:S(2)}) copy-start(f32[4096]{0:T(1024)} %param.13) | copy-start | bytes 49156
Sparse Core Ops, SparseCore 0:
  9.8 148.9 all-gather.1
  356.6 93.8 reduce-scatter.1
